TPU v7x, 32 devices: a whole 2x2x4 slice. The times are simulated.
32 devices in a mesh: row: 4 (over z), col: 8 (over y, x, core).
Axes of the slice: x: 2, y: 2, z: 4, core: 2. Of those that a mesh axis runs over, the one named last changes fastest.
Arguments:
- rho_real: float32 [4, 8, 1280000], P('row', 'col'), as said below
- rho_imag: float32 [4, 8, 1280000], P('row', 'col'), as said below
- cav_real: float32 [100, 100], replicated, may hold values from -0.4375 to 0.4375
- cav_imag: float32 [100, 100], replicated, may hold values from -0.4375 to 0.4375
- mech_real: float32 [64, 64], replicated, may hold values from -0.5 to 0.5
- mech_imag: float32 [64, 64], replicated, may hold values from -0.5 to 0.5
Outputs:
- out_real: float32 [4, 8, 1280000], P('row', 'col')
- out_imag: float32 [4, 8, 1280000], P('row', 'col')
Inputs may be any that keep to these rules, and one draw needn't show every extreme that they name: rho_real is the real part of a Hermitian matrix: symmetric in the whole matrix's row and column index. rho_imag is the imaginary part of a Hermitian matrix: antisymmetric in the whole matrix's row and column index.
All inputs are finite; a program needn't handle non-finite values.
Results may differ from a plain program's by a relative error of at most 0.0001.
Values sent between devices are 32-bit elements; how exact they have to be, the bound alone decides.
No kernel may reach another device: no remote copies, remote signals or barrier semaphores. Data moves between devices by JAX's collectives and lax.ppermute only.
A program may use at most 192 MiB of HBM per device.

v0:
```python
import jax
import jax.numpy as jnp
from jax import lax
from jax.sharding import PartitionSpec as P

MECH = 64
highest = lax.Precision.HIGHEST


def cavity_sides(parts, cav_real, cav_imag):
    real_part, imag_part = parts
    left_real = jnp.einsum("cd,mdne->mcne", cav_real, real_part, precision=highest) - jnp.einsum(
        "cd,mdne->mcne", cav_imag, imag_part, precision=highest
    )
    left_imag = jnp.einsum("cd,mdne->mcne", cav_real, imag_part, precision=highest) + jnp.einsum(
        "cd,mdne->mcne", cav_imag, real_part, precision=highest
    )
    right_real = jnp.einsum("mcne,fe->mcnf", left_real, cav_real, precision=highest) + jnp.einsum(
        "mcne,fe->mcnf", left_imag, cav_imag, precision=highest
    )
    right_imag = jnp.einsum("mcne,fe->mcnf", left_imag, cav_real, precision=highest) - jnp.einsum(
        "mcne,fe->mcnf", left_real, cav_imag, precision=highest
    )
    return (right_real, right_imag)


def mech_mix(pieces, mech_real, mech_imag, adjoint):
    real_part, imag_part = pieces
    plain_rr = jnp.einsum("mn,nok->mok", mech_real, real_part, precision=highest)
    plain_ii = jnp.einsum("mn,nok->mok", mech_imag, imag_part, precision=highest)
    plain_ri = jnp.einsum("mn,nok->mok", mech_real, imag_part, precision=highest)
    plain_ir = jnp.einsum("mn,nok->mok", mech_imag, real_part, precision=highest)
    if adjoint:
        return (plain_rr + plain_ii, plain_ri - plain_ir)
    return (plain_rr - plain_ii, plain_ri + plain_ir)


def ket_side(parts, mech_real, mech_imag):
    real_part, imag_part = parts
    local_rows, cav_count, local_cols, width = real_part.shape
    groups = lax.axis_size("row")
    flat = cav_count * local_cols * width
    shaped = (
        real_part.reshape(local_rows, groups, flat // groups),
        imag_part.reshape(local_rows, groups, flat // groups),
    )
    mixed = mech_mix(
        (
            lax.all_to_all(shaped[0], "row", split_axis=1, concat_axis=0, tiled=True),
            lax.all_to_all(shaped[1], "row", split_axis=1, concat_axis=0, tiled=True),
        ),
        mech_real,
        mech_imag,
        False,
    )
    return (
        lax.all_to_all(mixed[0], "row", split_axis=0, concat_axis=1, tiled=True).reshape(
            local_rows, cav_count, local_cols, width
        ),
        lax.all_to_all(mixed[1], "row", split_axis=0, concat_axis=1, tiled=True).reshape(
            local_rows, cav_count, local_cols, width
        ),
    )


def bra_side(parts, mech_real, mech_imag):
    real_part, imag_part = parts
    local_rows, cav_count, local_cols, width = real_part.shape
    groups = lax.axis_size("col")
    flat = local_rows * cav_count * width
    moved_real = jnp.transpose(real_part, (2, 0, 1, 3)).reshape(local_cols, groups, flat // groups)
    moved_imag = jnp.transpose(imag_part, (2, 0, 1, 3)).reshape(local_cols, groups, flat // groups)
    mixed = mech_mix(
        (
            lax.all_to_all(moved_real, "col", split_axis=1, concat_axis=0, tiled=True),
            lax.all_to_all(moved_imag, "col", split_axis=1, concat_axis=0, tiled=True),
        ),
        mech_real,
        mech_imag,
        True,
    )
    back_real = jnp.transpose(
        lax.all_to_all(mixed[0], "col", split_axis=0, concat_axis=1, tiled=True).reshape(
            local_cols, local_rows, cav_count, width
        ),
        (1, 2, 0, 3),
    )
    back_imag = jnp.transpose(
        lax.all_to_all(mixed[1], "col", split_axis=0, concat_axis=1, tiled=True).reshape(
            local_cols, local_rows, cav_count, width
        ),
        (1, 2, 0, 3),
    )
    return (back_real, back_imag)


def local(rho_real, rho_imag, cav_real, cav_imag, mech_real, mech_imag):
    block_shape = rho_real.shape
    cav_count = cav_real.shape[0]
    local_rows = MECH // lax.axis_size("row")
    local_cols = MECH // lax.axis_size("col")
    shape_four = (local_rows, cav_count, local_cols, cav_count)
    state = (rho_real.reshape(shape_four), rho_imag.reshape(shape_four))
    state = cavity_sides(state, cav_real, cav_imag)
    state = bra_side(ket_side(state, mech_real, mech_imag), mech_real, mech_imag)
    return (state[0].reshape(block_shape), state[1].reshape(block_shape))


def solution(mesh):
    return jax.shard_map(
        local,
        mesh=mesh,
        in_specs=(P("row", "col", None), P("row", "col", None), P(), P(), P(), P()),
        out_specs=(P("row", "col", None), P("row", "col", None)),
        check_vma=False,
    )
```

profile of v0, /device:TPU:0, one launch (start us, length us, event | category | flops | bytes accessed | tf_op | source)
XLA Modules:
  0.0 1057.0 jit_solution(15498159880655077600)
XLA Ops:
  1.2 41.2 %reduce.7 = f32[1280000]{0:T(1024)} reduce(f32[1,1,1280000]{2,1,0:T(1,128)} %param.6, f32[]{:T(128)} %broadcast.6), dimensions={0,1}, to_apply=%param.6.reduce_sub_computation.3 | reduce | bytes 10240004 | tf_op args[0]
  42.4 14.0 %reshape.80 = f32[16,100,8,100]{3,2,1,0:T(8,128)} reshape(f32[1280000]{0:T(1024)} %reduce.7) | data formatting | bytes 10240000 | tf_op jit(solution)/shard_map/reshape | solution.py:103
  64.6 41.2 %reduce.6 = f32[1280000]{0:T(1024)} reduce(f32[1,1,1280000]{2,1,0:T(1,128)} %param.7, f32[]{:T(128)} %broadcast.6), dimensions={0,1}, to_apply=%param.7.reduce_sub_computation.3 | reduce | bytes 10240004 | tf_op args[1]
  105.9 14.1 %reshape.81 = f32[16,100,8,100]{3,2,1,0:T(8,128)} reshape(f32[1280000]{0:T(1024)} %reduce.6) | data formatting | bytes 10240000 | tf_op jit(solution)/shard_map/reshape | solution.py:103
  156.3 17.2 %fusion.6 = f32[16,100,8,100]{3,1,2,0:T(8,128)} fusion(f32[16,8,100,100]{3,2,1,0:T(8,128)S(1)} %fusion.35, f32[16,8,100,100]{3,2,1,0:T(8,128)} %fusion.30, f32[100,100]{1,0:T(8,128)S(1)} %copy-done.6), kind=kOutput, calls=%fused_computation.10 | convolution fusion | flops 1537280000 | bytes 15400000 | tf_op jit(solution)/shard_map/mcne,fe->mcnf/dot_general | solution.py:18
  173.5 13.6 %fusion.22 = f32[16,100,8,100]{3,1,2,0:T(8,128)S(1)} fusion(f32[16,100,8,100]{3,1,2,0:T(8,128)} %fusion.6, f32[16,8,100,100]{3,2,1,0:T(8,128)S(1)} %fusion.38, f32[16,8,100,100]{3,2,1,0:T(8,128)S(1)} %fusion.32, f32[100,100]{1,0:T(8,128)S(1)} %copy-done), kind=kOutput, calls=%fused_computation.30 | convolution fusion | flops 1538560000 | bytes 20520000 | tf_op jit(solution)/shard_map/mcne,fe->mcnf/dot_general | solution.py:18
  210.8 14.5 %fusion.4 = f32[16,100,8,100]{3,1,2,0:T(8,128)S(1)} fusion(f32[16,8,100,100]{3,2,1,0:T(8,128)} %copy-done.4, f32[16,8,100,100]{3,2,1,0:T(8,128)} %fusion.30, f32[100,100]{1,0:T(8,128)S(1)} %copy-done), kind=kOutput, calls=%fused_computation.8 | convolution fusion | flops 1537280000 | bytes 15400000 | tf_op jit(solution)/shard_map/mcne,fe->mcnf/dot_general | solution.py:21
  225.4 14.1 %fusion.25 = f32[16,100,8,100]{3,1,2,0:T(8,128)S(1)} fusion(f32[16,100,8,100]{3,1,2,0:T(8,128)S(1)} %fusion.4, f32[16,8,100,100]{3,2,1,0:T(8,128)} %copy-done.5, f32[16,8,100,100]{3,2,1,0:T(8,128)S(1)} %bitcast.139, f32[100,100]{1,0:T(8,128)S(1)} %copy-done.6), kind=kOutput, calls=%fused_computation.31 | convolution fusion | flops 1538560000 | bytes 20520000 | tf_op jit(solution)/shard_map/mcne,fe->mcnf/dot_general | solution.py:21
  256.3 68.5 %all-to-all-done = f32[16,4,20000]{2,0,1:T(8,128)} async-done(((f32[16,4,20000]{2,0,1:T(8,128)}), f32[16,4,20000]{2,0,1:T(8,128)}, u32[]{:S(2)}, u32[]{:S(2)}) %all-to-all-start) | async-done | bytes 5120032 | tf_op jit(solution)/shard_map/all_to_all | solution.py:49
  329.9 9.6 fusion.40
  339.4 103.5 %all-to-all-done.1 = f32[16,4,20000]{2,0,1:T(8,128)} async-done(((f32[16,4,20000]{2,0,1:T(8,128)}), f32[16,4,20000]{2,0,1:T(8,128)}, u32[]{:S(2)}, u32[]{:S(2)}) %all-to-all-start.1) | async-done | bytes 5120032 | tf_op jit(solution)/shard_map/all_to_all | solution.py:50
  442.9 11.1 %fusion = f32[64,1,20000]{2,0,1:T(8,128)} fusion(f32[20000,64]{0,1:T(8,128)} %fusion.40, f32[64,20000]{1,0:T(8,128)} %bitcast.13, f32[64,64]{1,0:T(8,128)S(1)} %copy-done.8), kind=kOutput, calls=%fused_computation.4 | convolution fusion | flops 984320000 | bytes 15376384 | tf_op jit(solution)/shard_map/mn,nok->mok/dot_general | solution.py:30
  454.0 10.2 copy.70
  476.0 9.6 fusion.1
  485.6 10.0 copy.74
  495.6 86.9 %all-to-all-done.2 = f32[64,1,20000]{2,1,0:T(1,128)} async-done(((f32[64,1,20000]{2,1,0:T(1,128)}), f32[64,1,20000]{2,1,0:T(1,128)}, u32[]{:S(2)}, u32[]{:S(2)}) %all-to-all-start.2) | async-done | bytes 5120032 | tf_op jit(solution)/shard_map/all_to_all | solution.py:57
  622.7 78.3 %all-to-all-done.4 = f32[64,1,20000]{2,1,0:T(1,128)} async-done(((f32[64,1,20000]{2,1,0:T(1,128)}), f32[64,1,20000]{2,1,0:T(1,128)}, u32[]{:S(2)}, u32[]{:S(2)}) %all-to-all-start.4) | async-done | bytes 5120032 | tf_op jit(solution)/shard_map/all_to_all | solution.py:60
  740.6 24.3 %all-to-all-done.3 = f32[8,8,20000]{2,0,1:T(8,128)} async-done(((f32[8,8,20000]{2,0,1:T(8,128)}), f32[8,8,20000]{2,0,1:T(8,128)}, u32[]{:S(2)}, u32[]{:S(2)}) %all-to-all-start.3) | async-done | bytes 5120032 | tf_op jit(solution)/shard_map/all_to_all | solution.py:75
  769.8 9.5 fusion.13
  779.3 49.6 %all-to-all-done.5 = f32[8,8,20000]{2,0,1:T(8,128)} async-done(((f32[8,8,20000]{2,0,1:T(8,128)}), f32[8,8,20000]{2,0,1:T(8,128)}, u32[]{:S(2)}, u32[]{:S(2)}) %all-to-all-start.5) | async-done | bytes 5120032 | tf_op jit(solution)/shard_map/all_to_all | solution.py:76
  828.9 11.1 %fusion.2 = f32[64,1,20000]{2,0,1:T(8,128)} fusion(f32[20000,64]{0,1:T(8,128)} %fusion.13, f32[64,64]{1,0:T(8,128)S(1)} %copy-done.8, f32[8,8,20000]{2,0,1:T(8,128)} %all-to-all-done.5), kind=kOutput, calls=%fused_computation.6 | convolution fusion | flops 984320000 | bytes 15376384 | tf_op jit(solution)/shard_map/mn,nok->mok/dot_general | solution.py:30
  839.9 10.5 copy.78
  861.7 9.5 fusion.3
  871.3 10.1 copy.81
  881.3 33.0 %all-to-all-done.6 = f32[64,1,20000]{2,1,0:T(1,128)} async-done(((f32[64,1,20000]{2,1,0:T(1,128)}), f32[64,1,20000]{2,1,0:T(1,128)}, u32[]{:S(2)}, u32[]{:S(2)}) %all-to-all-start.6) | async-done | bytes 5120032 | tf_op jit(solution)/shard_map/all_to_all | solution.py:83
  924.7 53.6 %all-to-all-done.7 = f32[64,1,20000]{2,1,0:T(1,128)} async-done(((f32[64,1,20000]{2,1,0:T(1,128)}), f32[64,1,20000]{2,1,0:T(1,128)}, u32[]{:S(2)}, u32[]{:S(2)}) %all-to-all-start.7) | async-done | bytes 5120032 | tf_op jit(solution)/shard_map/all_to_all | solution.py:89
  984.0 9.2 reshape.94
  993.2 9.5 copy.83
  1002.8 17.6 %reshape.95 = f32[1,1,1280000]{2,1,0:T(1,128)} reshape(f32[16,100,8,100]{3,2,1,0:T(8,128)} %copy.83) | data formatting | bytes 10240000 | tf_op jit(solution)/shard_map/reshape | solution.py:106
  1020.4 9.0 reshape.92
  1029.4 9.5 copy.80
  1038.9 17.7 %reshape.93 = f32[1,1,1280000]{2,1,0:T(1,128)} reshape(f32[16,100,8,100]{3,2,1,0:T(8,128)} %copy.80) | data formatting | bytes 10240000 | tf_op jit(solution)/shard_map/reshape | solution.py:106
  (63 shorter events, 214.5 us)
Async XLA Ops:
  0.6 127.6 %copy-start = (f32[100,100]{1,0:T(8,128)S(1)}, f32[100,100]{1,0:T(8,128)}, u32[]{:S(2)}) copy-start(f32[100,100]{1,0:T(8,128)} %param.8) | copy-start | bytes 120004
  128.3 8.5 copy-start.2
  128.3 8.5 copy-start.6
  128.3 14.4 %slice-start = ((s8[6815744]{0:T(1024)(128)(4,1)}), s8[4194304]{0:T(1024)(128)(4,1)S(1)}, s32[]{:S(2)}) async-start(s8[6815744]{0:T(1024)(128)(4,1)} %bitcast.136), calls=%async_computation.8 | async-start | bytes 8388608
  136.8 19.4 %copy-start.4 = (f32[16,8,100,100]{3,2,1,0:T(8,128)}, f32[16,8,100,100]{3,2,1,0:T(8,128)S(1)}, u32[]{:S(2)}) copy-start(f32[16,8,100,100]{3,2,1,0:T(8,128)S(1)} %fusion.35) | copy-start | bytes 15360004
  136.8 5.9 slice-start.1
  142.7 30.8 %copy-start.3 = (f32[16,8,100,100]{3,2,1,0:T(8,128)}, f32[16,8,100,100]{3,2,1,0:T(8,128)S(1)}, u32[]{:S(2)}) copy-start(f32[16,8,100,100]{3,2,1,0:T(8,128)S(1)} %fusion.32) | copy-start | bytes 15360004
  156.3 17.3 %copy-start.5 = (f32[16,8,100,100]{3,2,1,0:T(8,128)}, f32[16,8,100,100]{3,2,1,0:T(8,128)S(1)}, u32[]{:S(2)}) copy-start(f32[16,8,100,100]{3,2,1,0:T(8,128)S(1)} %fusion.38) | copy-start | bytes 15360004
  204.0 21.3 %slice-start.2 = ((s8[6815744]{0:T(1024)(128)(4,1)}), s8[2621440]{0:T(1024)(128)(4,1)S(1)}, s32[]{:S(2)}) async-start(s8[6815744]{0:T(1024)(128)(4,1)} %bitcast.138), calls=%async_computation.10 | async-start | bytes 5242880
  204.0 120.8 %all-to-all-start = ((f32[16,4,20000]{2,0,1:T(8,128)}), f32[16,4,20000]{2,0,1:T(8,128)}, u32[]{:S(2)}, u32[]{:S(2)}) async-start(f32[16,4,20000]{2,0,1:T(8,128)} %copy.65), calls=%async_computation | async-start | bytes 10289152 | tf_op jit(solution)/shard_map/all_to_all | solution.py:49
  210.8 14.5 %slice-start.3 = ((s8[6815744]{0:T(1024)(128)(4,1)}), s8[4194304]{0:T(1024)(128)(4,1)S(1)}, s32[]{:S(2)}) async-start(s8[6815744]{0:T(1024)(128)(4,1)} %bitcast.138), calls=%async_computation.11 | async-start | bytes 8388608
  256.3 73.5 %copy-start.7 = (f32[64,64]{1,0:T(8,128)S(1)}, f32[64,64]{1,0:T(8,128)}, u32[]{:S(2)}) copy-start(f32[64,64]{1,0:T(8,128)} %param.10) | copy-start | bytes 49156
  324.8 118.1 %all-to-all-start.1 = ((f32[16,4,20000]{2,0,1:T(8,128)}), f32[16,4,20000]{2,0,1:T(8,128)}, u32[]{:S(2)}, u32[]{:S(2)}) async-start(f32[16,4,20000]{2,0,1:T(8,128)} %copy.69), calls=%async_computation.1 | async-start | bytes 10289152 | tf_op jit(solution)/shard_map/all_to_all | solution.py:50
  329.8 113.1 %copy-start.8 = (f32[64,64]{1,0:T(8,128)S(1)}, f32[64,64]{1,0:T(8,128)}, u32[]{:S(2)}) copy-start(f32[64,64]{1,0:T(8,128)} %param.11) | copy-start | bytes 49156
  464.3 118.2 %all-to-all-start.2 = ((f32[64,1,20000]{2,1,0:T(1,128)}), f32[64,1,20000]{2,1,0:T(1,128)}, u32[]{:S(2)}, u32[]{:S(2)}) async-start(f32[64,1,20000]{2,1,0:T(1,128)} %copy.70), calls=%async_computation.2 | async-start | bytes 10289152 | tf_op jit(solution)/shard_map/all_to_all | solution.py:57
  582.4 118.5 %all-to-all-start.4 = ((f32[64,1,20000]{2,1,0:T(1,128)}), f32[64,1,20000]{2,1,0:T(1,128)}, u32[]{:S(2)}, u32[]{:S(2)}) async-start(f32[64,1,20000]{2,1,0:T(1,128)} %copy.74), calls=%async_computation.4 | async-start | bytes 10289152 | tf_op jit(solution)/shard_map/all_to_all | solution.py:60
  701.0 64.0 %all-to-all-start.3 = ((f32[8,8,20000]{2,0,1:T(8,128)}), f32[8,8,20000]{2,0,1:T(8,128)}, u32[]{:S(2)}, u32[]{:S(2)}) async-start(f32[8,8,20000]{2,0,1:T(8,128)} %copy.73), calls=%async_computation.3 | async-start | bytes 10289152 | tf_op jit(solution)/shard_map/all_to_all | solution.py:75
  764.9 63.9 %all-to-all-start.5 = ((f32[8,8,20000]{2,0,1:T(8,128)}), f32[8,8,20000]{2,0,1:T(8,128)}, u32[]{:S(2)}, u32[]{:S(2)}) async-start(f32[8,8,20000]{2,0,1:T(8,128)} %copy.77), calls=%async_computation.5 | async-start | bytes 10289152 | tf_op jit(solution)/shard_map/all_to_all | solution.py:76
  850.4 63.9 %all-to-all-start.6 = ((f32[64,1,20000]{2,1,0:T(1,128)}), f32[64,1,20000]{2,1,0:T(1,128)}, u32[]{:S(2)}, u32[]{:S(2)}) async-start(f32[64,1,20000]{2,1,0:T(1,128)} %copy.78), calls=%async_computation.6 | async-start | bytes 10289152 | tf_op jit(solution)/shard_map/all_to_all | solution.py:83
  914.3 64.0 %all-to-all-start.7 = ((f32[64,1,20000]{2,1,0:T(1,128)}), f32[64,1,20000]{2,1,0:T(1,128)}, u32[]{:S(2)}, u32[]{:S(2)}) async-start(f32[64,1,20000]{2,1,0:T(1,128)} %copy.81), calls=%async_computation.7 | async-start | bytes 10289152 | tf_op jit(solution)/shard_map/all_to_all | solution.py:89
  1029.4 27.2 %copy-start.1 = (f32[100,100]{1,0:T(8,128)S(1)}, f32[100,100]{1,0:T(8,128)}, u32[]{:S(2)}) copy-start(f32[100,100]{1,0:T(8,128)} %param.8) | copy-start | bytes 120004
where the time goes:
time: 1070 us; the launch traced here: 1060 us
  waiting for transfers between devices  498 us (47%)
  local copies, waits for them, and re-layouts  274 us (26%)
  matrix products  161 us (15%)
  other arithmetic  82.4 us (8%)
  starting transfers between devices  41.1 us (4%)
    all_to_all x1, waiting for transfers between devices, ket_side(): lax.all_to_all(shaped[1], 'row', split_axis=1, concat_axis=0, tiled=True)  103 us
    all_to_all x1, waiting for transfers between devices, ket_side(): lax.all_to_all(mixed[0], 'row', split_axis=0, concat_axis=1, tiled=True)  86.9 us
    unnamed x4, other arithmetic  82.4 us
    all_to_all x1, waiting for transfers between devices, ket_side(): lax.all_to_all(mixed[1], 'row', split_axis=0, concat_axis=1, tiled=True)  78.3 us
    all_to_all x1, waiting for transfers between devices, ket_side(): lax.all_to_all(shaped[0], 'row', split_axis=1, concat_axis=0, tiled=True)  68.5 us
    all_to_all x1, waiting for transfers between devices, bra_side(): lax.all_to_all(mixed[1], 'col', split_axis=0, concat_axis=1, tiled=True)  53.6 us
    all_to_all x1, waiting for transfers between devices, bra_side(): lax.all_to_all(moved_imag, 'col', split_axis=1, concat_axis=0, tiled=True)  49.6 us
    reshape x4, local copies, waits for them, and re-layouts, local(): state = (rho_real.reshape(shape_four), rho_imag.reshape(shape_four))  44.6 us
  transfers between devices with their start and end apart: 8, of which 8 were waited for; matrix products, arithmetic and copies ran while one was open for 18% of the time, Pallas kernels for 0%

commit v1 on v0

--- a/solution.py
+++ b/solution.py
@@ -86,9 +86,12 @@
         (1, 2, 0, 3),
     )
     back_imag = jnp.transpose(
-        lax.all_to_all(mixed[1], "col", split_axis=0, concat_axis=1, tiled=True).reshape(
-            local_cols, local_rows, cav_count, width
-        ),
+        jnp.concatenate(
+            lax.all_to_all(
+                jnp.stack(jnp.split(mixed[1], lax.axis_size("col"), axis=0)), "col", 0, 0
+            ),
+            axis=1,
+        ).reshape(local_cols, local_rows, cav_count, width),
         (1, 2, 0, 3),
     )
     return (back_real, back_imag)

time: 1070 us -> 1030 us (0.963)
  waiting for transfers between devices: 498 us -> 467 us
    all_to_all x1, waiting for transfers between devices: 53.6 us -> 17 us  [bra_side(): lax.all_to_all(jnp.stack(jnp.split(mixed[1], lax.axis_size('col'), axis=0...]
  transfers between devices with their start and end apart: 8 -> 8, of which waited for: 8 -> 8; matrix products, arithmetic and copies ran while one was open for 18% -> 22% of each run, Pallas kernels for 0% -> 0%
where the time goes in v1:
time: 1030 us; the launch traced here: 1020 us
  waiting for transfers between devices  467 us (45%)
  local copies, waits for them, and re-layouts  271 us (26%)
  matrix products  158 us (15%)
  other arithmetic  82.4 us (8%)
  starting transfers between devices  41.1 us (4%)
    all_to_all x1, waiting for transfers between devices, ket_side(): lax.all_to_all(shaped[1], 'row', split_axis=1, concat_axis=0, tiled=True)  103 us
    all_to_all x1, waiting for transfers between devices, ket_side(): lax.all_to_all(mixed[0], 'row', split_axis=0, concat_axis=1, tiled=True)  86.9 us
    unnamed x4, other arithmetic  82.4 us
    all_to_all x1, waiting for transfers between devices, ket_side(): lax.all_to_all(mixed[1], 'row', split_axis=0, concat_axis=1, tiled=True)  78.3 us
    all_to_all x1, waiting for transfers between devices, ket_side(): lax.all_to_all(shaped[0], 'row', split_axis=1, concat_axis=0, tiled=True)  68.5 us
    all_to_all x1, waiting for transfers between devices, bra_side(): lax.all_to_all(moved_imag, 'col', split_axis=1, concat_axis=0, tiled=True)  49.6 us
    reshape x4, local copies, waits for them, and re-layouts, local(): state = (rho_real.reshape(shape_four), rho_imag.reshape(shape_four))  44.6 us
    all_to_all x1, waiting for transfers between devices, bra_side(): lax.all_to_all(mixed[0], 'col', split_axis=0, concat_axis=1, tiled=True)  38.8 us
  transfers between devices with their start and end apart: 8, of which 8 were waited for; matrix products, arithmetic and copies ran while one was open for 22% of the time, Pallas kernels for 0%

profile of v1, /device:TPU:0, one launch (start us, length us, event | category | flops | bytes accessed | tf_op | source)
XLA Modules:
  0.0 1020.5 jit_solution(1211714638985155818)
XLA Ops:
  1.2 41.2 %reduce.7 = f32[1280000]{0:T(1024)} reduce(f32[1,1,1280000]{2,1,0:T(1,128)} %param.6, f32[]{:T(128)} %broadcast.6), dimensions={0,1}, to_apply=%param.6.reduce_sub_computation.3 | reduce | bytes 10240004 | tf_op args[0]
  42.4 14.0 %reshape.95 = f32[16,100,8,100]{3,2,1,0:T(8,128)} reshape(f32[1280000]{0:T(1024)} %reduce.7) | data formatting | bytes 10240000 | tf_op jit(solution)/shard_map/reshape | solution.py:106
  64.6 41.2 %reduce.6 = f32[1280000]{0:T(1024)} reduce(f32[1,1,1280000]{2,1,0:T(1,128)} %param.7, f32[]{:T(128)} %broadcast.6), dimensions={0,1}, to_apply=%param.7.reduce_sub_computation.3 | reduce | bytes 10240004 | tf_op args[1]
  105.9 14.1 %reshape.96 = f32[16,100,8,100]{3,2,1,0:T(8,128)} reshape(f32[1280000]{0:T(1024)} %reduce.6) | data formatting | bytes 10240000 | tf_op jit(solution)/shard_map/reshape | solution.py:106
  156.3 17.2 %fusion.6 = f32[16,100,8,100]{3,1,2,0:T(8,128)} fusion(f32[16,8,100,100]{3,2,1,0:T(8,128)S(1)} %fusion.43, f32[16,8,100,100]{3,2,1,0:T(8,128)} %fusion.38, f32[100,100]{1,0:T(8,128)S(1)} %copy-done.6), kind=kOutput, calls=%fused_computation.10 | convolution fusion | flops 1537280000 | bytes 15400000 | tf_op jit(solution)/shard_map/mcne,fe->mcnf/dot_general | solution.py:18
  173.5 13.6 %fusion.22 = f32[16,100,8,100]{3,1,2,0:T(8,128)S(1)} fusion(f32[16,100,8,100]{3,1,2,0:T(8,128)} %fusion.6, f32[16,8,100,100]{3,2,1,0:T(8,128)S(1)} %fusion.46, f32[16,8,100,100]{3,2,1,0:T(8,128)S(1)} %fusion.40, f32[100,100]{1,0:T(8,128)S(1)} %copy-done), kind=kOutput, calls=%fused_computation.29 | convolution fusion | flops 1538560000 | bytes 20520000 | tf_op jit(solution)/shard_map/mcne,fe->mcnf/dot_general | solution.py:18
  210.8 14.5 %fusion.4 = f32[16,100,8,100]{3,1,2,0:T(8,128)S(1)} fusion(f32[16,8,100,100]{3,2,1,0:T(8,128)} %copy-done.4, f32[16,8,100,100]{3,2,1,0:T(8,128)} %fusion.38, f32[100,100]{1,0:T(8,128)S(1)} %copy-done), kind=kOutput, calls=%fused_computation.8 | convolution fusion | flops 1537280000 | bytes 15400000 | tf_op jit(solution)/shard_map/mcne,fe->mcnf/dot_general | solution.py:21
  225.4 14.1 %fusion.25 = f32[16,100,8,100]{3,1,2,0:T(8,128)S(1)} fusion(f32[16,100,8,100]{3,1,2,0:T(8,128)S(1)} %fusion.4, f32[16,8,100,100]{3,2,1,0:T(8,128)} %copy-done.5, f32[16,8,100,100]{3,2,1,0:T(8,128)S(1)} %bitcast.166, f32[100,100]{1,0:T(8,128)S(1)} %copy-done.6), kind=kOutput, calls=%fused_computation.30 | convolution fusion | flops 1538560000 | bytes 20520000 | tf_op jit(solution)/shard_map/mcne,fe->mcnf/dot_general | solution.py:21
  256.3 68.5 %all-to-all-done = f32[16,4,20000]{2,0,1:T(8,128)} async-done(((f32[16,4,20000]{2,0,1:T(8,128)}), f32[16,4,20000]{2,0,1:T(8,128)}, u32[]{:S(2)}, u32[]{:S(2)}) %all-to-all-start) | async-done | bytes 5120032 | tf_op jit(solution)/shard_map/all_to_all | solution.py:49
  329.9 9.6 fusion.48
  339.4 103.5 %all-to-all-done.1 = f32[16,4,20000]{2,0,1:T(8,128)} async-done(((f32[16,4,20000]{2,0,1:T(8,128)}), f32[16,4,20000]{2,0,1:T(8,128)}, u32[]{:S(2)}, u32[]{:S(2)}) %all-to-all-start.1) | async-done | bytes 5120032 | tf_op jit(solution)/shard_map/all_to_all | solution.py:50
  442.9 11.1 %fusion = f32[64,1,20000]{2,0,1:T(8,128)} fusion(f32[20000,64]{0,1:T(8,128)} %fusion.48, f32[64,20000]{1,0:T(8,128)} %bitcast.13, f32[64,64]{1,0:T(8,128)S(1)} %copy-done.8), kind=kOutput, calls=%fused_computation.4 | convolution fusion | flops 984320000 | bytes 15376384 | tf_op jit(solution)/shard_map/mn,nok->mok/dot_general | solution.py:30
  454.0 10.2 %copy.70 = f32[64,1,20000]{2,1,0:T(1,128)} copy(f32[64,1,20000]{2,0,1:T(8,128)} %fusion) | data formatting | bytes 10240000 | tf_op jit(solution)/shard_map/sub | solution.py:35
  476.0 9.6 fusion.1
  485.6 10.0 copy.74
  495.6 86.9 %all-to-all-done.2 = f32[64,1,20000]{2,1,0:T(1,128)} async-done(((f32[64,1,20000]{2,1,0:T(1,128)}), f32[64,1,20000]{2,1,0:T(1,128)}, u32[]{:S(2)}, u32[]{:S(2)}) %all-to-all-start.2) | async-done | bytes 5120032 | tf_op jit(solution)/shard_map/all_to_all | solution.py:57
  594.6 8.6 reshape.101
  622.7 78.3 %all-to-all-done.4 = f32[64,1,20000]{2,1,0:T(1,128)} async-done(((f32[64,1,20000]{2,1,0:T(1,128)}), f32[64,1,20000]{2,1,0:T(1,128)}, u32[]{:S(2)}, u32[]{:S(2)}) %all-to-all-start.4) | async-done | bytes 5120032 | tf_op jit(solution)/shard_map/all_to_all | solution.py:60
  712.4 8.6 reshape.104
  740.6 24.3 %all-to-all-done.3 = f32[8,8,20000]{2,0,1:T(8,128)} async-done(((f32[8,8,20000]{2,0,1:T(8,128)}), f32[8,8,20000]{2,0,1:T(8,128)}, u32[]{:S(2)}, u32[]{:S(2)}) %all-to-all-start.3) | async-done | bytes 5120032 | tf_op jit(solution)/shard_map/all_to_all | solution.py:75
  769.8 9.5 fusion.13
  779.3 49.6 %all-to-all-done.5 = f32[8,8,20000]{2,0,1:T(8,128)} async-done(((f32[8,8,20000]{2,0,1:T(8,128)}), f32[8,8,20000]{2,0,1:T(8,128)}, u32[]{:S(2)}, u32[]{:S(2)}) %all-to-all-start.5) | async-done | bytes 5120032 | tf_op jit(solution)/shard_map/all_to_all | solution.py:76
  828.9 11.1 %fusion.2 = f32[64,1,20000]{2,0,1:T(8,128)} fusion(f32[20000,64]{0,1:T(8,128)} %fusion.13, f32[64,64]{1,0:T(8,128)S(1)} %copy-done.8, f32[8,8,20000]{2,0,1:T(8,128)} %all-to-all-done.5), kind=kOutput, calls=%fused_computation.6 | convolution fusion | flops 984320000 | bytes 15376384 | tf_op jit(solution)/shard_map/mn,nok->mok/dot_general | solution.py:30
  839.9 10.3 %copy.78 = f32[64,1,20000]{2,1,0:T(1,128)} copy(f32[64,1,20000]{2,0,1:T(8,128)} %fusion.2) | data formatting | bytes 10240000 | tf_op jit(solution)/shard_map/add | solution.py:34
  875.4 38.8 %all-to-all-done.6 = f32[64,1,20000]{2,1,0:T(1,128)} async-done(((f32[64,1,20000]{2,1,0:T(1,128)}), f32[64,1,20000]{2,1,0:T(1,128)}, u32[]{:S(2)}, u32[]{:S(2)}) %all-to-all-start.6) | async-done | bytes 5120032 | tf_op jit(solution)/shard_map/all_to_all | solution.py:83
  924.6 9.4 reshape.107
  934.0 9.5 copy.80
  943.5 17.6 %reshape.108 = f32[1,1,1280000]{2,1,0:T(1,128)} reshape(f32[16,100,8,100]{3,2,1,0:T(8,128)} %copy.80) | data formatting | bytes 10240000 | tf_op jit(solution)/shard_map/reshape | solution.py:109
  961.1 17.0 %all-to-all-done.7 = f32[8,8,1,20000]{3,1,2,0:T(8,128)} async-done(((f32[8,8,1,20000]{3,1,2,0:T(8,128)}), f32[8,8,1,20000]{3,1,2,0:T(8,128)}, u32[]{:S(2)}, u32[]{:S(2)}) %all-to-all-start.7) | async-done | bytes 5120032 | tf_op jit(solution)/shard_map/all_to_all | solution.py:90
  983.8 9.2 reshape_reshape.3
  993.1 9.5 copy.82
  1002.6 17.7 %reshape.110 = f32[1,1,1280000]{2,1,0:T(1,128)} reshape(f32[16,100,8,100]{3,2,1,0:T(8,128)} %copy.82) | data formatting | bytes 10240000 | tf_op jit(solution)/shard_map/reshape | solution.py:109
  (70 shorter events, 211.0 us)
Async XLA Ops:
  0.6 127.6 %copy-start = (f32[100,100]{1,0:T(8,128)S(1)}, f32[100,100]{1,0:T(8,128)}, u32[]{:S(2)}) copy-start(f32[100,100]{1,0:T(8,128)} %param.8) | copy-start | bytes 120004
  128.3 8.5 copy-start.2
  128.3 8.5 copy-start.6
  128.3 14.4 %slice-start = ((s8[6815744]{0:T(1024)(128)(4,1)}), s8[4194304]{0:T(1024)(128)(4,1)S(1)}, s32[]{:S(2)}) async-start(s8[6815744]{0:T(1024)(128)(4,1)} %bitcast.163), calls=%async_computation.8 | async-start | bytes 8388608
  136.8 19.4 %copy-start.4 = (f32[16,8,100,100]{3,2,1,0:T(8,128)}, f32[16,8,100,100]{3,2,1,0:T(8,128)S(1)}, u32[]{:S(2)}) copy-start(f32[16,8,100,100]{3,2,1,0:T(8,128)S(1)} %fusion.43) | copy-start | bytes 15360004
  136.8 5.9 slice-start.1
  142.7 30.8 %copy-start.3 = (f32[16,8,100,100]{3,2,1,0:T(8,128)}, f32[16,8,100,100]{3,2,1,0:T(8,128)S(1)}, u32[]{:S(2)}) copy-start(f32[16,8,100,100]{3,2,1,0:T(8,128)S(1)} %fusion.40) | copy-start | bytes 15360004
  156.3 17.3 %copy-start.5 = (f32[16,8,100,100]{3,2,1,0:T(8,128)}, f32[16,8,100,100]{3,2,1,0:T(8,128)S(1)}, u32[]{:S(2)}) copy-start(f32[16,8,100,100]{3,2,1,0:T(8,128)S(1)} %fusion.46) | copy-start | bytes 15360004
  204.0 21.3 %slice-start.2 = ((s8[6815744]{0:T(1024)(128)(4,1)}), s8[2621440]{0:T(1024)(128)(4,1)S(1)}, s32[]{:S(2)}) async-start(s8[6815744]{0:T(1024)(128)(4,1)} %bitcast.165), calls=%async_computation.10 | async-start | bytes 5242880
  204.0 120.8 %all-to-all-start = ((f32[16,4,20000]{2,0,1:T(8,128)}), f32[16,4,20000]{2,0,1:T(8,128)}, u32[]{:S(2)}, u32[]{:S(2)}) async-start(f32[16,4,20000]{2,0,1:T(8,128)} %copy.65), calls=%async_computation | async-start | bytes 10289152 | tf_op jit(solution)/shard_map/all_to_all | solution.py:49
  210.8 14.5 %slice-start.3 = ((s8[6815744]{0:T(1024)(128)(4,1)}), s8[4194304]{0:T(1024)(128)(4,1)S(1)}, s32[]{:S(2)}) async-start(s8[6815744]{0:T(1024)(128)(4,1)} %bitcast.165), calls=%async_computation.11 | async-start | bytes 8388608
  256.3 73.5 %copy-start.7 = (f32[64,64]{1,0:T(8,128)S(1)}, f32[64,64]{1,0:T(8,128)}, u32[]{:S(2)}) copy-start(f32[64,64]{1,0:T(8,128)} %param.10) | copy-start | bytes 49156
  324.8 118.1 %all-to-all-start.1 = ((f32[16,4,20000]{2,0,1:T(8,128)}), f32[16,4,20000]{2,0,1:T(8,128)}, u32[]{:S(2)}, u32[]{:S(2)}) async-start(f32[16,4,20000]{2,0,1:T(8,128)} %copy.69), calls=%async_computation.1 | async-start | bytes 10289152 | tf_op jit(solution)/shard_map/all_to_all | solution.py:50
  329.8 113.1 %copy-start.8 = (f32[64,64]{1,0:T(8,128)S(1)}, f32[64,64]{1,0:T(8,128)}, u32[]{:S(2)}) copy-start(f32[64,64]{1,0:T(8,128)} %param.11) | copy-start | bytes 49156
  464.3 118.2 %all-to-all-start.2 = ((f32[64,1,20000]{2,1,0:T(1,128)}), f32[64,1,20000]{2,1,0:T(1,128)}, u32[]{:S(2)}, u32[]{:S(2)}) async-start(f32[64,1,20000]{2,1,0:T(1,128)} %copy.70), calls=%async_computation.2 | async-start | bytes 10289152 | tf_op jit(solution)/shard_map/all_to_all | solution.py:57
  582.4 118.5 %all-to-all-start.4 = ((f32[64,1,20000]{2,1,0:T(1,128)}), f32[64,1,20000]{2,1,0:T(1,128)}, u32[]{:S(2)}, u32[]{:S(2)}) async-start(f32[64,1,20000]{2,1,0:T(1,128)} %copy.74), calls=%async_computation.4 | async-start | bytes 10289152 | tf_op jit(solution)/shard_map/all_to_all | solution.py:60
  701.0 64.0 %all-to-all-start.3 = ((f32[8,8,20000]{2,0,1:T(8,128)}), f32[8,8,20000]{2,0,1:T(8,128)}, u32[]{:S(2)}, u32[]{:S(2)}) async-start(f32[8,8,20000]{2,0,1:T(8,128)} %copy.73), calls=%async_computation.3 | async-start | bytes 10289152 | tf_op jit(solution)/shard_map/all_to_all | solution.py:75
  764.9 64.0 %all-to-all-start.5 = ((f32[8,8,20000]{2,0,1:T(8,128)}), f32[8,8,20000]{2,0,1:T(8,128)}, u32[]{:S(2)}, u32[]{:S(2)}) async-start(f32[8,8,20000]{2,0,1:T(8,128)} %copy.77), calls=%async_computation.5 | async-start | bytes 10289152 | tf_op jit(solution)/shard_map/all_to_all | solution.py:76
  850.2 63.9 %all-to-all-start.6 = ((f32[64,1,20000]{2,1,0:T(1,128)}), f32[64,1,20000]{2,1,0:T(1,128)}, u32[]{:S(2)}, u32[]{:S(2)}) async-start(f32[64,1,20000]{2,1,0:T(1,128)} %copy.78), calls=%async_computation.6 | async-start | bytes 10289152 | tf_op jit(solution)/shard_map/all_to_all | solution.py:83
  914.1 64.0 %all-to-all-start.7 = ((f32[8,8,1,20000]{3,1,2,0:T(8,128)}), f32[8,8,1,20000]{3,1,2,0:T(8,128)}, u32[]{:S(2)}, u32[]{:S(2)}) async-start(f32[8,8,1,20000]{3,1,2,0:T(8,128)} %fusion.28), calls=%async_computation.7 | async-start | bytes 10289152 | tf_op jit(solution)/shard_map/all_to_all | solution.py:90
  993.1 27.2 %copy-start.1 = (f32[100,100]{1,0:T(8,128)S(1)}, f32[100,100]{1,0:T(8,128)}, u32[]{:S(2)}) copy-start(f32[100,100]{1,0:T(8,128)} %param.8) | copy-start | bytes 120004
